TPU v7x, 256 devices: a whole 4x4x8 slice. The times are simulated.
256 devices in a mesh: seq: 32 (over y, x, core), head: 8 (over z).
Axes of the slice: x: 4, y: 4, z: 8, core: 2. Of those that a mesh axis runs over, the one named last changes fastest.
Arguments:
- queries: bfloat16 [32768, 8192], P(('seq', 'head')), may hold values from -6 to 6
- key_vectors: bfloat16 [32768, 8192], P(('seq', 'head')), may hold values from -6 to 6
- value_vectors: bfloat16 [32768, 8192], P(('seq', 'head')), may hold values from -6 to 6
- out_gain: float32 [64, 128], P('head'), may hold values from 0.1 to 1.9
Outputs:
- attended: bfloat16 [32768, 8192], P(('seq', 'head'))
All inputs are finite; a program needn't handle non-finite values.
Results may differ from a plain program's by a relative error of at most 0.0049.
Values may be sent and summed in bfloat16 or wider, within the bound.
A program may use at most 128 MiB of HBM per device.

v0:
```python
import jax
import jax.numpy as jnp
from jax import lax
from jax.sharding import PartitionSpec as P

HEADS = 64
HD = 128
BLOCK = 512


def passed_along(block, axis, distance):
    devices = range(lax.axis_size(axis))
    route = [(i - distance, i) for i in devices if i - distance in devices]
    return lax.ppermute(block, axis, route)


def split_heads(matrix):
    return matrix.reshape(matrix.shape[0], HEADS, HD)


def to_blocks(tensor):
    return tensor.reshape(tensor.shape[0] // BLOCK, BLOCK, tensor.shape[1], HD)


def block_states(key_heads, value_heads):
    return jnp.einsum(
        "nbhd,nbhe->nhde",
        to_blocks(key_heads),
        to_blocks(value_heads),
        preferred_element_type=jnp.float32,
    )


def carried_states(states):
    own = jnp.sum(states, axis=0)
    seq_count = lax.axis_size("seq")

    def relay(step, prefix):
        return passed_along(prefix + own, "seq", 1)

    prefix = lax.fori_loop(0, seq_count - 1, relay, jnp.zeros_like(own))
    carried = prefix[None] + (jnp.cumsum(states, axis=0) - states)
    return carried.astype(jnp.bfloat16)


def per_device(queries, key_vectors, value_vectors, out_gain):
    query_heads, key_heads, value_heads = (
        lax.all_to_all(split_heads(queries), "head", split_axis=1, concat_axis=0, tiled=True),
        lax.all_to_all(split_heads(key_vectors), "head", split_axis=1, concat_axis=0, tiled=True),
        lax.all_to_all(split_heads(value_vectors), "head", split_axis=1, concat_axis=0, tiled=True),
    )
    carried = carried_states(block_states(key_heads, value_heads))
    query_blocks = to_blocks(query_heads)
    key_blocks = to_blocks(key_heads)
    value_blocks = to_blocks(value_heads)
    inter = jnp.einsum("nbhd,nhde->nbhe", query_blocks, carried, preferred_element_type=jnp.float32)
    scores = jnp.einsum(
        "nbhd,nchd->nhbc", query_blocks, key_blocks, preferred_element_type=jnp.float32
    )
    causal = jnp.arange(BLOCK)[:, None] >= jnp.arange(BLOCK)[None, :]
    scores = jnp.where(causal[None, None], scores, jnp.float32(0.0)).astype(jnp.bfloat16)
    intra = jnp.einsum("nhbc,nchd->nbhd", scores, value_blocks, preferred_element_type=jnp.float32)
    raw = inter + intra
    scale = lax.rsqrt(jnp.mean(raw * raw, axis=-1, keepdims=True) + 1e-06)
    normed = (raw * scale * out_gain[None, None]).astype(jnp.bfloat16)
    normed = normed.reshape(query_heads.shape[0], query_heads.shape[1], HD)
    tokens_back = lax.all_to_all(normed, "head", split_axis=0, concat_axis=1, tiled=True)
    return tokens_back.reshape(tokens_back.shape[0], HEADS * HD)


def solution(mesh):
    return jax.shard_map(
        per_device,
        mesh=mesh,
        in_specs=(
            P(("seq", "head"), None),
            P(("seq", "head"), None),
            P(("seq", "head"), None),
            P("head", None),
        ),
        out_specs=P(("seq", "head"), None),
        check_vma=False,
    )
```

profile of v0, /device:TPU:16, one launch (start us, length us, event | category | flops | bytes accessed | tf_op | source)
XLA Modules:
  0.0 646.3 jit_solution(1137800084721814047)
XLA Ops:
  22.7 43.1 %all-to-all-done = bf16[128,64,128]{2,0,1:T(8,128)(2,1)S(1)} async-done(((bf16[128,64,128]{2,0,1:T(8,128)(2,1)}), bf16[128,64,128]{2,0,1:T(8,128)(2,1)S(1)}, u32[]{:S(2)}, u32[]{:S(2)}) %all-to-all-start) | async-done | bytes 2097184 | tf_op jit(solution)/shard_map/all_to_all | solution.py:49
  78.3 43.5 %all-to-all-done.1 = bf16[128,64,128]{2,0,1:T(8,128)(2,1)} async-done(((bf16[128,64,128]{2,0,1:T(8,128)(2,1)}), bf16[128,64,128]{2,0,1:T(8,128)(2,1)}, u32[]{:S(2)}, u32[]{:S(2)}) %all-to-all-start.1) | async-done | bytes 2097184 | tf_op jit(solution)/shard_map/all_to_all | solution.py:50
  132.0 43.0 %all-to-all-done.2 = bf16[128,64,128]{2,0,1:T(8,128)(2,1)} async-done(((bf16[128,64,128]{2,0,1:T(8,128)(2,1)}), bf16[128,64,128]{2,0,1:T(8,128)(2,1)}, u32[]{:S(2)}, u32[]{:S(2)}) %all-to-all-start.2) | async-done | bytes 2097184 | tf_op jit(solution)/shard_map/all_to_all | solution.py:48
  181.6 392.8 %while.10 = (s32[]{:T(128)}, f32[8,128,128]{2,1,0:T(8,128)S(1)}, f32[8,128,128]{2,1,0:T(8,128)S(1)}, s32[]{:T(128)}) while((s32[]{:T(128)}, f32[8,128,128]{2,1,0:T(8,128)S(1)}, f32[8,128,128]{2,1,0:T(8,128)S(1)}, s32[]{:T(128)}) %tuple.20), condition=%wide.region_2.0_spmd, body=%wide.region_1.0_spmd.sunk | while | flops 131074 | bytes 3670109 | solution.py:41
  183.6 10.7 %collective-permute-done = f32[8,128,128]{2,1,0:T(8,128)S(1)} collective-permute-done((f32[8,128,128]{2,1,0:T(8,128)S(1)}, f32[8,128,128]{2,1,0:T(8,128)S(1)}, u32[]{:S(2)}, u32[]{:S(2)}) %collective-permute-start) | collective-permute-done | bytes 524320 | tf_op jit(solution)/shard_map/while/body/eval_jaxpr/ppermute | solution.py:14
  196.3 10.7 %collective-permute-done = f32[8,128,128]{2,1,0:T(8,128)S(1)} collective-permute-done((f32[8,128,128]{2,1,0:T(8,128)S(1)}, f32[8,128,128]{2,1,0:T(8,128)S(1)}, u32[]{:S(2)}, u32[]{:S(2)}) %collective-permute-start) | collective-permute-done | bytes 524320 | tf_op jit(solution)/shard_map/while/body/eval_jaxpr/ppermute | solution.py:14
  209.0 10.7 %collective-permute-done = f32[8,128,128]{2,1,0:T(8,128)S(1)} collective-permute-done((f32[8,128,128]{2,1,0:T(8,128)S(1)}, f32[8,128,128]{2,1,0:T(8,128)S(1)}, u32[]{:S(2)}, u32[]{:S(2)}) %collective-permute-start) | collective-permute-done | bytes 524320 | tf_op jit(solution)/shard_map/while/body/eval_jaxpr/ppermute | solution.py:14
  221.6 10.7 %collective-permute-done = f32[8,128,128]{2,1,0:T(8,128)S(1)} collective-permute-done((f32[8,128,128]{2,1,0:T(8,128)S(1)}, f32[8,128,128]{2,1,0:T(8,128)S(1)}, u32[]{:S(2)}, u32[]{:S(2)}) %collective-permute-start) | collective-permute-done | bytes 524320 | tf_op jit(solution)/shard_map/while/body/eval_jaxpr/ppermute | solution.py:14
  234.3 10.7 %collective-permute-done = f32[8,128,128]{2,1,0:T(8,128)S(1)} collective-permute-done((f32[8,128,128]{2,1,0:T(8,128)S(1)}, f32[8,128,128]{2,1,0:T(8,128)S(1)}, u32[]{:S(2)}, u32[]{:S(2)}) %collective-permute-start) | collective-permute-done | bytes 524320 | tf_op jit(solution)/shard_map/while/body/eval_jaxpr/ppermute | solution.py:14
  247.0 10.7 %collective-permute-done = f32[8,128,128]{2,1,0:T(8,128)S(1)} collective-permute-done((f32[8,128,128]{2,1,0:T(8,128)S(1)}, f32[8,128,128]{2,1,0:T(8,128)S(1)}, u32[]{:S(2)}, u32[]{:S(2)}) %collective-permute-start) | collective-permute-done | bytes 524320 | tf_op jit(solution)/shard_map/while/body/eval_jaxpr/ppermute | solution.py:14
  259.7 10.7 %collective-permute-done = f32[8,128,128]{2,1,0:T(8,128)S(1)} collective-permute-done((f32[8,128,128]{2,1,0:T(8,128)S(1)}, f32[8,128,128]{2,1,0:T(8,128)S(1)}, u32[]{:S(2)}, u32[]{:S(2)}) %collective-permute-start) | collective-permute-done | bytes 524320 | tf_op jit(solution)/shard_map/while/body/eval_jaxpr/ppermute | solution.py:14
  272.3 10.7 %collective-permute-done = f32[8,128,128]{2,1,0:T(8,128)S(1)} collective-permute-done((f32[8,128,128]{2,1,0:T(8,128)S(1)}, f32[8,128,128]{2,1,0:T(8,128)S(1)}, u32[]{:S(2)}, u32[]{:S(2)}) %collective-permute-start) | collective-permute-done | bytes 524320 | tf_op jit(solution)/shard_map/while/body/eval_jaxpr/ppermute | solution.py:14
  285.0 10.7 %collective-permute-done = f32[8,128,128]{2,1,0:T(8,128)S(1)} collective-permute-done((f32[8,128,128]{2,1,0:T(8,128)S(1)}, f32[8,128,128]{2,1,0:T(8,128)S(1)}, u32[]{:S(2)}, u32[]{:S(2)}) %collective-permute-start) | collective-permute-done | bytes 524320 | tf_op jit(solution)/shard_map/while/body/eval_jaxpr/ppermute | solution.py:14
  297.7 10.7 %collective-permute-done = f32[8,128,128]{2,1,0:T(8,128)S(1)} collective-permute-done((f32[8,128,128]{2,1,0:T(8,128)S(1)}, f32[8,128,128]{2,1,0:T(8,128)S(1)}, u32[]{:S(2)}, u32[]{:S(2)}) %collective-permute-start) | collective-permute-done | bytes 524320 | tf_op jit(solution)/shard_map/while/body/eval_jaxpr/ppermute | solution.py:14
  310.3 10.7 %collective-permute-done = f32[8,128,128]{2,1,0:T(8,128)S(1)} collective-permute-done((f32[8,128,128]{2,1,0:T(8,128)S(1)}, f32[8,128,128]{2,1,0:T(8,128)S(1)}, u32[]{:S(2)}, u32[]{:S(2)}) %collective-permute-start) | collective-permute-done | bytes 524320 | tf_op jit(solution)/shard_map/while/body/eval_jaxpr/ppermute | solution.py:14
  323.0 10.7 %collective-permute-done = f32[8,128,128]{2,1,0:T(8,128)S(1)} collective-permute-done((f32[8,128,128]{2,1,0:T(8,128)S(1)}, f32[8,128,128]{2,1,0:T(8,128)S(1)}, u32[]{:S(2)}, u32[]{:S(2)}) %collective-permute-start) | collective-permute-done | bytes 524320 | tf_op jit(solution)/shard_map/while/body/eval_jaxpr/ppermute | solution.py:14
  335.7 10.7 %collective-permute-done = f32[8,128,128]{2,1,0:T(8,128)S(1)} collective-permute-done((f32[8,128,128]{2,1,0:T(8,128)S(1)}, f32[8,128,128]{2,1,0:T(8,128)S(1)}, u32[]{:S(2)}, u32[]{:S(2)}) %collective-permute-start) | collective-permute-done | bytes 524320 | tf_op jit(solution)/shard_map/while/body/eval_jaxpr/ppermute | solution.py:14
  348.3 10.7 %collective-permute-done = f32[8,128,128]{2,1,0:T(8,128)S(1)} collective-permute-done((f32[8,128,128]{2,1,0:T(8,128)S(1)}, f32[8,128,128]{2,1,0:T(8,128)S(1)}, u32[]{:S(2)}, u32[]{:S(2)}) %collective-permute-start) | collective-permute-done | bytes 524320 | tf_op jit(solution)/shard_map/while/body/eval_jaxpr/ppermute | solution.py:14
  361.0 10.7 %collective-permute-done = f32[8,128,128]{2,1,0:T(8,128)S(1)} collective-permute-done((f32[8,128,128]{2,1,0:T(8,128)S(1)}, f32[8,128,128]{2,1,0:T(8,128)S(1)}, u32[]{:S(2)}, u32[]{:S(2)}) %collective-permute-start) | collective-permute-done | bytes 524320 | tf_op jit(solution)/shard_map/while/body/eval_jaxpr/ppermute | solution.py:14
  373.7 10.7 %collective-permute-done = f32[8,128,128]{2,1,0:T(8,128)S(1)} collective-permute-done((f32[8,128,128]{2,1,0:T(8,128)S(1)}, f32[8,128,128]{2,1,0:T(8,128)S(1)}, u32[]{:S(2)}, u32[]{:S(2)}) %collective-permute-start) | collective-permute-done | bytes 524320 | tf_op jit(solution)/shard_map/while/body/eval_jaxpr/ppermute | solution.py:14
  386.4 10.7 %collective-permute-done = f32[8,128,128]{2,1,0:T(8,128)S(1)} collective-permute-done((f32[8,128,128]{2,1,0:T(8,128)S(1)}, f32[8,128,128]{2,1,0:T(8,128)S(1)}, u32[]{:S(2)}, u32[]{:S(2)}) %collective-permute-start) | collective-permute-done | bytes 524320 | tf_op jit(solution)/shard_map/while/body/eval_jaxpr/ppermute | solution.py:14
  399.0 10.7 %collective-permute-done = f32[8,128,128]{2,1,0:T(8,128)S(1)} collective-permute-done((f32[8,128,128]{2,1,0:T(8,128)S(1)}, f32[8,128,128]{2,1,0:T(8,128)S(1)}, u32[]{:S(2)}, u32[]{:S(2)}) %collective-permute-start) | collective-permute-done | bytes 524320 | tf_op jit(solution)/shard_map/while/body/eval_jaxpr/ppermute | solution.py:14
  411.7 10.7 %collective-permute-done = f32[8,128,128]{2,1,0:T(8,128)S(1)} collective-permute-done((f32[8,128,128]{2,1,0:T(8,128)S(1)}, f32[8,128,128]{2,1,0:T(8,128)S(1)}, u32[]{:S(2)}, u32[]{:S(2)}) %collective-permute-start) | collective-permute-done | bytes 524320 | tf_op jit(solution)/shard_map/while/body/eval_jaxpr/ppermute | solution.py:14
  594.1 46.0 %all_to_all.60 = bf16[1024,8,128]{2,1,0:T(8,128)(2,1)} all-to-all(bf16[1024,8,128]{2,1,0:T(8,128)(2,1)S(1)} %bitcast.27), channel_id=1, replica_groups=mesh['seq'=32,'head'=8] {'head'}, dimensions={0} | all-to-all | bytes 4194304 | tf_op jit(solution)/shard_map/all_to_all | solution.py:67
  (105 shorter events, 267.2 us)
Async XLA Ops:
  6.1 59.7 %all-to-all-start = ((bf16[128,64,128]{2,0,1:T(8,128)(2,1)}), bf16[128,64,128]{2,0,1:T(8,128)(2,1)S(1)}, u32[]{:S(2)}, u32[]{:S(2)}) async-start(bf16[128,64,128]{2,0,1:T(8,128)(2,1)} %copy.46), calls=%async_computation | async-start | bytes 4194304 | tf_op jit(solution)/shard_map/all_to_all | solution.py:49
  65.8 56.0 %all-to-all-start.1 = ((bf16[128,64,128]{2,0,1:T(8,128)(2,1)}), bf16[128,64,128]{2,0,1:T(8,128)(2,1)}, u32[]{:S(2)}, u32[]{:S(2)}) async-start(bf16[128,64,128]{2,0,1:T(8,128)(2,1)} %copy.50), calls=%async_computation.1 | async-start | bytes 4194304 | tf_op jit(solution)/shard_map/all_to_all | solution.py:50
  121.8 53.2 %all-to-all-start.2 = ((bf16[128,64,128]{2,0,1:T(8,128)(2,1)}), bf16[128,64,128]{2,0,1:T(8,128)(2,1)}, u32[]{:S(2)}, u32[]{:S(2)}) async-start(bf16[128,64,128]{2,0,1:T(8,128)(2,1)} %copy.56), calls=%async_computation.2 | async-start | bytes 4194304 | tf_op jit(solution)/shard_map/all_to_all | solution.py:48
  181.7 12.6 %collective-permute-start = (f32[8,128,128]{2,1,0:T(8,128)S(1)}, f32[8,128,128]{2,1,0:T(8,128)S(1)}, u32[]{:S(2)}, u32[]{:S(2)}) collective-permute-start(f32[8,128,128]{2,1,0:T(8,128)S(1)} %add.43), channel_id=1, source_target_pairs={{0,8},{8,16},{16,24},{24,32},{32,40},{40,48},{48,56},{56,64},{64,7... | collective-permute-start | bytes 1572872 | tf_op jit(solution)/shard_map/while/body/eval_jaxpr/ppermute | solution.py:14
  194.4 12.6 %collective-permute-start = (f32[8,128,128]{2,1,0:T(8,128)S(1)}, f32[8,128,128]{2,1,0:T(8,128)S(1)}, u32[]{:S(2)}, u32[]{:S(2)}) collective-permute-start(f32[8,128,128]{2,1,0:T(8,128)S(1)} %add.43), channel_id=1, source_target_pairs={{0,8},{8,16},{16,24},{24,32},{32,40},{40,48},{48,56},{56,64},{64,7... | collective-permute-start | bytes 1572872 | tf_op jit(solution)/shard_map/while/body/eval_jaxpr/ppermute | solution.py:14
  207.0 12.6 %collective-permute-start = (f32[8,128,128]{2,1,0:T(8,128)S(1)}, f32[8,128,128]{2,1,0:T(8,128)S(1)}, u32[]{:S(2)}, u32[]{:S(2)}) collective-permute-start(f32[8,128,128]{2,1,0:T(8,128)S(1)} %add.43), channel_id=1, source_target_pairs={{0,8},{8,16},{16,24},{24,32},{32,40},{40,48},{48,56},{56,64},{64,7... | collective-permute-start | bytes 1572872 | tf_op jit(solution)/shard_map/while/body/eval_jaxpr/ppermute | solution.py:14
  219.7 12.6 %collective-permute-start = (f32[8,128,128]{2,1,0:T(8,128)S(1)}, f32[8,128,128]{2,1,0:T(8,128)S(1)}, u32[]{:S(2)}, u32[]{:S(2)}) collective-permute-start(f32[8,128,128]{2,1,0:T(8,128)S(1)} %add.43), channel_id=1, source_target_pairs={{0,8},{8,16},{16,24},{24,32},{32,40},{40,48},{48,56},{56,64},{64,7... | collective-permute-start | bytes 1572872 | tf_op jit(solution)/shard_map/while/body/eval_jaxpr/ppermute | solution.py:14
  232.4 12.6 %collective-permute-start = (f32[8,128,128]{2,1,0:T(8,128)S(1)}, f32[8,128,128]{2,1,0:T(8,128)S(1)}, u32[]{:S(2)}, u32[]{:S(2)}) collective-permute-start(f32[8,128,128]{2,1,0:T(8,128)S(1)} %add.43), channel_id=1, source_target_pairs={{0,8},{8,16},{16,24},{24,32},{32,40},{40,48},{48,56},{56,64},{64,7... | collective-permute-start | bytes 1572872 | tf_op jit(solution)/shard_map/while/body/eval_jaxpr/ppermute | solution.py:14
  245.1 12.6 %collective-permute-start = (f32[8,128,128]{2,1,0:T(8,128)S(1)}, f32[8,128,128]{2,1,0:T(8,128)S(1)}, u32[]{:S(2)}, u32[]{:S(2)}) collective-permute-start(f32[8,128,128]{2,1,0:T(8,128)S(1)} %add.43), channel_id=1, source_target_pairs={{0,8},{8,16},{16,24},{24,32},{32,40},{40,48},{48,56},{56,64},{64,7... | collective-permute-start | bytes 1572872 | tf_op jit(solution)/shard_map/while/body/eval_jaxpr/ppermute | solution.py:14
  257.7 12.6 %collective-permute-start = (f32[8,128,128]{2,1,0:T(8,128)S(1)}, f32[8,128,128]{2,1,0:T(8,128)S(1)}, u32[]{:S(2)}, u32[]{:S(2)}) collective-permute-start(f32[8,128,128]{2,1,0:T(8,128)S(1)} %add.43), channel_id=1, source_target_pairs={{0,8},{8,16},{16,24},{24,32},{32,40},{40,48},{48,56},{56,64},{64,7... | collective-permute-start | bytes 1572872 | tf_op jit(solution)/shard_map/while/body/eval_jaxpr/ppermute | solution.py:14
  270.4 12.6 %collective-permute-start = (f32[8,128,128]{2,1,0:T(8,128)S(1)}, f32[8,128,128]{2,1,0:T(8,128)S(1)}, u32[]{:S(2)}, u32[]{:S(2)}) collective-permute-start(f32[8,128,128]{2,1,0:T(8,128)S(1)} %add.43), channel_id=1, source_target_pairs={{0,8},{8,16},{16,24},{24,32},{32,40},{40,48},{48,56},{56,64},{64,7... | collective-permute-start | bytes 1572872 | tf_op jit(solution)/shard_map/while/body/eval_jaxpr/ppermute | solution.py:14
  283.1 12.6 %collective-permute-start = (f32[8,128,128]{2,1,0:T(8,128)S(1)}, f32[8,128,128]{2,1,0:T(8,128)S(1)}, u32[]{:S(2)}, u32[]{:S(2)}) collective-permute-start(f32[8,128,128]{2,1,0:T(8,128)S(1)} %add.43), channel_id=1, source_target_pairs={{0,8},{8,16},{16,24},{24,32},{32,40},{40,48},{48,56},{56,64},{64,7... | collective-permute-start | bytes 1572872 | tf_op jit(solution)/shard_map/while/body/eval_jaxpr/ppermute | solution.py:14
  295.7 12.6 %collective-permute-start = (f32[8,128,128]{2,1,0:T(8,128)S(1)}, f32[8,128,128]{2,1,0:T(8,128)S(1)}, u32[]{:S(2)}, u32[]{:S(2)}) collective-permute-start(f32[8,128,128]{2,1,0:T(8,128)S(1)} %add.43), channel_id=1, source_target_pairs={{0,8},{8,16},{16,24},{24,32},{32,40},{40,48},{48,56},{56,64},{64,7... | collective-permute-start | bytes 1572872 | tf_op jit(solution)/shard_map/while/body/eval_jaxpr/ppermute | solution.py:14
  308.4 12.6 %collective-permute-start = (f32[8,128,128]{2,1,0:T(8,128)S(1)}, f32[8,128,128]{2,1,0:T(8,128)S(1)}, u32[]{:S(2)}, u32[]{:S(2)}) collective-permute-start(f32[8,128,128]{2,1,0:T(8,128)S(1)} %add.43), channel_id=1, source_target_pairs={{0,8},{8,16},{16,24},{24,32},{32,40},{40,48},{48,56},{56,64},{64,7... | collective-permute-start | bytes 1572872 | tf_op jit(solution)/shard_map/while/body/eval_jaxpr/ppermute | solution.py:14
  321.1 12.6 %collective-permute-start = (f32[8,128,128]{2,1,0:T(8,128)S(1)}, f32[8,128,128]{2,1,0:T(8,128)S(1)}, u32[]{:S(2)}, u32[]{:S(2)}) collective-permute-start(f32[8,128,128]{2,1,0:T(8,128)S(1)} %add.43), channel_id=1, source_target_pairs={{0,8},{8,16},{16,24},{24,32},{32,40},{40,48},{48,56},{56,64},{64,7... | collective-permute-start | bytes 1572872 | tf_op jit(solution)/shard_map/while/body/eval_jaxpr/ppermute | solution.py:14
  333.7 12.6 %collective-permute-start = (f32[8,128,128]{2,1,0:T(8,128)S(1)}, f32[8,128,128]{2,1,0:T(8,128)S(1)}, u32[]{:S(2)}, u32[]{:S(2)}) collective-permute-start(f32[8,128,128]{2,1,0:T(8,128)S(1)} %add.43), channel_id=1, source_target_pairs={{0,8},{8,16},{16,24},{24,32},{32,40},{40,48},{48,56},{56,64},{64,7... | collective-permute-start | bytes 1572872 | tf_op jit(solution)/shard_map/while/body/eval_jaxpr/ppermute | solution.py:14
  346.4 12.6 %collective-permute-start = (f32[8,128,128]{2,1,0:T(8,128)S(1)}, f32[8,128,128]{2,1,0:T(8,128)S(1)}, u32[]{:S(2)}, u32[]{:S(2)}) collective-permute-start(f32[8,128,128]{2,1,0:T(8,128)S(1)} %add.43), channel_id=1, source_target_pairs={{0,8},{8,16},{16,24},{24,32},{32,40},{40,48},{48,56},{56,64},{64,7... | collective-permute-start | bytes 1572872 | tf_op jit(solution)/shard_map/while/body/eval_jaxpr/ppermute | solution.py:14
  359.1 12.6 %collective-permute-start = (f32[8,128,128]{2,1,0:T(8,128)S(1)}, f32[8,128,128]{2,1,0:T(8,128)S(1)}, u32[]{:S(2)}, u32[]{:S(2)}) collective-permute-start(f32[8,128,128]{2,1,0:T(8,128)S(1)} %add.43), channel_id=1, source_target_pairs={{0,8},{8,16},{16,24},{24,32},{32,40},{40,48},{48,56},{56,64},{64,7... | collective-permute-start | bytes 1572872 | tf_op jit(solution)/shard_map/while/body/eval_jaxpr/ppermute | solution.py:14
  371.8 12.6 %collective-permute-start = (f32[8,128,128]{2,1,0:T(8,128)S(1)}, f32[8,128,128]{2,1,0:T(8,128)S(1)}, u32[]{:S(2)}, u32[]{:S(2)}) collective-permute-start(f32[8,128,128]{2,1,0:T(8,128)S(1)} %add.43), channel_id=1, source_target_pairs={{0,8},{8,16},{16,24},{24,32},{32,40},{40,48},{48,56},{56,64},{64,7... | collective-permute-start | bytes 1572872 | tf_op jit(solution)/shard_map/while/body/eval_jaxpr/ppermute | solution.py:14
  384.4 12.6 %collective-permute-start = (f32[8,128,128]{2,1,0:T(8,128)S(1)}, f32[8,128,128]{2,1,0:T(8,128)S(1)}, u32[]{:S(2)}, u32[]{:S(2)}) collective-permute-start(f32[8,128,128]{2,1,0:T(8,128)S(1)} %add.43), channel_id=1, source_target_pairs={{0,8},{8,16},{16,24},{24,32},{32,40},{40,48},{48,56},{56,64},{64,7... | collective-permute-start | bytes 1572872 | tf_op jit(solution)/shard_map/while/body/eval_jaxpr/ppermute | solution.py:14
  397.1 12.6 %collective-permute-start = (f32[8,128,128]{2,1,0:T(8,128)S(1)}, f32[8,128,128]{2,1,0:T(8,128)S(1)}, u32[]{:S(2)}, u32[]{:S(2)}) collective-permute-start(f32[8,128,128]{2,1,0:T(8,128)S(1)} %add.43), channel_id=1, source_target_pairs={{0,8},{8,16},{16,24},{24,32},{32,40},{40,48},{48,56},{56,64},{64,7... | collective-permute-start | bytes 1572872 | tf_op jit(solution)/shard_map/while/body/eval_jaxpr/ppermute | solution.py:14
  409.8 12.6 %collective-permute-start = (f32[8,128,128]{2,1,0:T(8,128)S(1)}, f32[8,128,128]{2,1,0:T(8,128)S(1)}, u32[]{:S(2)}, u32[]{:S(2)}) collective-permute-start(f32[8,128,128]{2,1,0:T(8,128)S(1)} %add.43), channel_id=1, source_target_pairs={{0,8},{8,16},{16,24},{24,32},{32,40},{40,48},{48,56},{56,64},{64,7... | collective-permute-start | bytes 1572872 | tf_op jit(solution)/shard_map/while/body/eval_jaxpr/ppermute | solution.py:14
  422.4 12.6 %collective-permute-start = (f32[8,128,128]{2,1,0:T(8,128)S(1)}, f32[8,128,128]{2,1,0:T(8,128)S(1)}, u32[]{:S(2)}, u32[]{:S(2)}) collective-permute-start(f32[8,128,128]{2,1,0:T(8,128)S(1)} %add.43), channel_id=1, source_target_pairs={{0,8},{8,16},{16,24},{24,32},{32,40},{40,48},{48,56},{56,64},{64,7... | collective-permute-start | bytes 1572872 | tf_op jit(solution)/shard_map/while/body/eval_jaxpr/ppermute | solution.py:14
  435.1 12.6 %collective-permute-start = (f32[8,128,128]{2,1,0:T(8,128)S(1)}, f32[8,128,128]{2,1,0:T(8,128)S(1)}, u32[]{:S(2)}, u32[]{:S(2)}) collective-permute-start(f32[8,128,128]{2,1,0:T(8,128)S(1)} %add.43), channel_id=1, source_target_pairs={{0,8},{8,16},{16,24},{24,32},{32,40},{40,48},{48,56},{56,64},{64,7... | collective-permute-start | bytes 1572872 | tf_op jit(solution)/shard_map/while/body/eval_jaxpr/ppermute | solution.py:14
  (14 other events, 183.5 us)
where the time goes:
time: 648 us; the launch traced here: 646 us
  waiting for transfers between devices  461 us (71%)
  starting transfers between devices  76.7 us (12%)
  blocking collectives  46 us (7%)
  local copies, waits for them, and re-layouts  42.2 us (7%)
  matrix products  14.6 us (2%)
    ppermute x31, waiting for transfers between devices, passed_along(): return lax.ppermute(block, axis, route)  331 us
    ppermute x31, starting transfers between devices, passed_along(): return lax.ppermute(block, axis, route)  59.5 us
    all_to_all x1, blocking collectives, per_device(): lax.all_to_all(normed, 'head', split_axis=0, concat_axis=1, tiled=True)  46 us
    all_to_all x1, waiting for transfers between devices, per_device(): lax.all_to_all(split_heads(value_vectors), 'head', split_axis=1, concat_a...  43.5 us
    all_to_all x1, waiting for transfers between devices, per_device(): lax.all_to_all(split_heads(key_vectors), 'head', split_axis=1, concat_axi...  43.1 us
    all_to_all x1, waiting for transfers between devices, per_device(): lax.all_to_all(split_heads(queries), 'head', split_axis=1, concat_axis=0,...  43 us
  transfers between devices with their start and end apart: 34, of which 34 were waited for; matrix products, arithmetic and copies ran while one was open for 3% of the time, Pallas kernels for 0%

commit v1 on v0

--- a/solution.py
+++ b/solution.py
@@ -47,7 +47,15 @@
     query_heads, key_heads, value_heads = (
         lax.all_to_all(split_heads(queries), "head", split_axis=1, concat_axis=0, tiled=True),
         lax.all_to_all(split_heads(key_vectors), "head", split_axis=1, concat_axis=0, tiled=True),
-        lax.all_to_all(split_heads(value_vectors), "head", split_axis=1, concat_axis=0, tiled=True),
+        jnp.concatenate(
+            lax.all_to_all(
+                jnp.stack(jnp.split(split_heads(value_vectors), lax.axis_size("head"), axis=1)),
+                "head",
+                0,
+                0,
+            ),
+            axis=0,
+        ),
     )
     carried = carried_states(block_states(key_heads, value_heads))
     query_blocks = to_blocks(query_heads)

time: 648 us -> 611 us (0.943)
  waiting for transfers between devices: 461 us -> 418 us
    all_to_all x1, waiting for transfers between devices: 43 us -> 0.01 us  [per_device(): lax.all_to_all(split_heads(queries), 'head', split_axis=1, concat_axis=0,...]
    unnamed x11 -> x22, local copies, waits for them, and re-layouts: 11.7 us -> 17.1 us
  transfers between devices with their start and end apart: 34 -> 34, of which waited for: 34 -> 33; matrix products, arithmetic and copies ran while one was open for 3% -> 4% of each run, Pallas kernels for 0% -> 0%
where the time goes in v1:
time: 611 us; the launch traced here: 609 us
  waiting for transfers between devices  418 us (68%)
  starting transfers between devices  76.9 us (13%)
  blocking collectives  49.4 us (8%)
  local copies, waits for them, and re-layouts  46.6 us (8%)
  matrix products  13.8 us (2%)
    ppermute x31, waiting for transfers between devices, passed_along(): return lax.ppermute(block, axis, route)  331 us
    ppermute x31, starting transfers between devices, passed_along(): return lax.ppermute(block, axis, route)  59.5 us
    all_to_all x1, blocking collectives, per_device(): lax.all_to_all(normed, 'head', split_axis=0, concat_axis=1, tiled=True)  49.4 us
    all_to_all x1, waiting for transfers between devices, per_device(): lax.all_to_all(split_heads(key_vectors), 'head', split_axis=1, concat_axi...  43.5 us
    all_to_all x1, waiting for transfers between devices, per_device(): lax.all_to_all(jnp.stack(jnp.split(split_heads(value_vectors), lax.axis_s...  43.1 us
    unnamed x22, local copies, waits for them, and re-layouts  17.1 us
  transfers between devices with their start and end apart: 34, of which 33 were waited for; matrix products, arithmetic and copies ran while one was open for 4% of the time, Pallas kernels for 0%

profile of v1, /device:TPU:16, one launch (start us, length us, event | category | flops | bytes accessed | tf_op | source)
XLA Modules:
  0.0 609.5 jit_solution(1342917815631152329)
XLA Ops:
  25.0 43.1 %all-to-all-done = bf16[8,128,8,128]{3,2,1,0:T(8,128)(2,1)S(1)} async-done(((bf16[8,128,8,128]{3,2,1,0:T(8,128)(2,1)}), bf16[8,128,8,128]{3,2,1,0:T(8,128)(2,1)S(1)}, u32[]{:S(2)}, u32[]{:S(2)}) %all-to-all-start) | async-done | bytes 2097184 | tf_op jit(solution)/shard_map/all_to_all | solution.py:51
  80.5 43.5 %all-to-all-done.1 = bf16[128,64,128]{2,0,1:T(8,128)(2,1)} async-done(((bf16[128,64,128]{2,0,1:T(8,128)(2,1)}), bf16[128,64,128]{2,0,1:T(8,128)(2,1)}, u32[]{:S(2)}, u32[]{:S(2)}) %all-to-all-start.1) | async-done | bytes 2097184 | tf_op jit(solution)/shard_map/all_to_all | solution.py:49
  135.9 392.8 %while.10 = (s32[]{:T(128)}, f32[8,128,128]{2,1,0:T(8,128)S(1)}, f32[8,128,128]{2,1,0:T(8,128)S(1)}, s32[]{:T(128)}) while((s32[]{:T(128)}, f32[8,128,128]{2,1,0:T(8,128)S(1)}, f32[8,128,128]{2,1,0:T(8,128)S(1)}, s32[]{:T(128)}) %tuple.22), condition=%wide.region_2.0_spmd, body=%wide.region_1.0_spmd.sunk | while | flops 131074 | bytes 3670109 | solution.py:41
  137.9 10.7 %collective-permute-done = f32[8,128,128]{2,1,0:T(8,128)S(1)} collective-permute-done((f32[8,128,128]{2,1,0:T(8,128)S(1)}, f32[8,128,128]{2,1,0:T(8,128)S(1)}, u32[]{:S(2)}, u32[]{:S(2)}) %collective-permute-start) | collective-permute-done | bytes 524320 | tf_op jit(solution)/shard_map/while/body/eval_jaxpr/ppermute | solution.py:14
  150.6 10.7 %collective-permute-done = f32[8,128,128]{2,1,0:T(8,128)S(1)} collective-permute-done((f32[8,128,128]{2,1,0:T(8,128)S(1)}, f32[8,128,128]{2,1,0:T(8,128)S(1)}, u32[]{:S(2)}, u32[]{:S(2)}) %collective-permute-start) | collective-permute-done | bytes 524320 | tf_op jit(solution)/shard_map/while/body/eval_jaxpr/ppermute | solution.py:14
  163.3 10.7 %collective-permute-done = f32[8,128,128]{2,1,0:T(8,128)S(1)} collective-permute-done((f32[8,128,128]{2,1,0:T(8,128)S(1)}, f32[8,128,128]{2,1,0:T(8,128)S(1)}, u32[]{:S(2)}, u32[]{:S(2)}) %collective-permute-start) | collective-permute-done | bytes 524320 | tf_op jit(solution)/shard_map/while/body/eval_jaxpr/ppermute | solution.py:14
  175.9 10.7 %collective-permute-done = f32[8,128,128]{2,1,0:T(8,128)S(1)} collective-permute-done((f32[8,128,128]{2,1,0:T(8,128)S(1)}, f32[8,128,128]{2,1,0:T(8,128)S(1)}, u32[]{:S(2)}, u32[]{:S(2)}) %collective-permute-start) | collective-permute-done | bytes 524320 | tf_op jit(solution)/shard_map/while/body/eval_jaxpr/ppermute | solution.py:14
  188.6 10.7 %collective-permute-done = f32[8,128,128]{2,1,0:T(8,128)S(1)} collective-permute-done((f32[8,128,128]{2,1,0:T(8,128)S(1)}, f32[8,128,128]{2,1,0:T(8,128)S(1)}, u32[]{:S(2)}, u32[]{:S(2)}) %collective-permute-start) | collective-permute-done | bytes 524320 | tf_op jit(solution)/shard_map/while/body/eval_jaxpr/ppermute | solution.py:14
  201.3 10.7 %collective-permute-done = f32[8,128,128]{2,1,0:T(8,128)S(1)} collective-permute-done((f32[8,128,128]{2,1,0:T(8,128)S(1)}, f32[8,128,128]{2,1,0:T(8,128)S(1)}, u32[]{:S(2)}, u32[]{:S(2)}) %collective-permute-start) | collective-permute-done | bytes 524320 | tf_op jit(solution)/shard_map/while/body/eval_jaxpr/ppermute | solution.py:14
  214.0 10.7 %collective-permute-done = f32[8,128,128]{2,1,0:T(8,128)S(1)} collective-permute-done((f32[8,128,128]{2,1,0:T(8,128)S(1)}, f32[8,128,128]{2,1,0:T(8,128)S(1)}, u32[]{:S(2)}, u32[]{:S(2)}) %collective-permute-start) | collective-permute-done | bytes 524320 | tf_op jit(solution)/shard_map/while/body/eval_jaxpr/ppermute | solution.py:14
  226.6 10.7 %collective-permute-done = f32[8,128,128]{2,1,0:T(8,128)S(1)} collective-permute-done((f32[8,128,128]{2,1,0:T(8,128)S(1)}, f32[8,128,128]{2,1,0:T(8,128)S(1)}, u32[]{:S(2)}, u32[]{:S(2)}) %collective-permute-start) | collective-permute-done | bytes 524320 | tf_op jit(solution)/shard_map/while/body/eval_jaxpr/ppermute | solution.py:14
  239.3 10.7 %collective-permute-done = f32[8,128,128]{2,1,0:T(8,128)S(1)} collective-permute-done((f32[8,128,128]{2,1,0:T(8,128)S(1)}, f32[8,128,128]{2,1,0:T(8,128)S(1)}, u32[]{:S(2)}, u32[]{:S(2)}) %collective-permute-start) | collective-permute-done | bytes 524320 | tf_op jit(solution)/shard_map/while/body/eval_jaxpr/ppermute | solution.py:14
  252.0 10.7 %collective-permute-done = f32[8,128,128]{2,1,0:T(8,128)S(1)} collective-permute-done((f32[8,128,128]{2,1,0:T(8,128)S(1)}, f32[8,128,128]{2,1,0:T(8,128)S(1)}, u32[]{:S(2)}, u32[]{:S(2)}) %collective-permute-start) | collective-permute-done | bytes 524320 | tf_op jit(solution)/shard_map/while/body/eval_jaxpr/ppermute | solution.py:14
  264.6 10.7 %collective-permute-done = f32[8,128,128]{2,1,0:T(8,128)S(1)} collective-permute-done((f32[8,128,128]{2,1,0:T(8,128)S(1)}, f32[8,128,128]{2,1,0:T(8,128)S(1)}, u32[]{:S(2)}, u32[]{:S(2)}) %collective-permute-start) | collective-permute-done | bytes 524320 | tf_op jit(solution)/shard_map/while/body/eval_jaxpr/ppermute | solution.py:14
  277.3 10.7 %collective-permute-done = f32[8,128,128]{2,1,0:T(8,128)S(1)} collective-permute-done((f32[8,128,128]{2,1,0:T(8,128)S(1)}, f32[8,128,128]{2,1,0:T(8,128)S(1)}, u32[]{:S(2)}, u32[]{:S(2)}) %collective-permute-start) | collective-permute-done | bytes 524320 | tf_op jit(solution)/shard_map/while/body/eval_jaxpr/ppermute | solution.py:14
  290.0 10.7 %collective-permute-done = f32[8,128,128]{2,1,0:T(8,128)S(1)} collective-permute-done((f32[8,128,128]{2,1,0:T(8,128)S(1)}, f32[8,128,128]{2,1,0:T(8,128)S(1)}, u32[]{:S(2)}, u32[]{:S(2)}) %collective-permute-start) | collective-permute-done | bytes 524320 | tf_op jit(solution)/shard_map/while/body/eval_jaxpr/ppermute | solution.py:14
  302.6 10.7 %collective-permute-done = f32[8,128,128]{2,1,0:T(8,128)S(1)} collective-permute-done((f32[8,128,128]{2,1,0:T(8,128)S(1)}, f32[8,128,128]{2,1,0:T(8,128)S(1)}, u32[]{:S(2)}, u32[]{:S(2)}) %collective-permute-start) | collective-permute-done | bytes 524320 | tf_op jit(solution)/shard_map/while/body/eval_jaxpr/ppermute | solution.py:14
  315.3 10.7 %collective-permute-done = f32[8,128,128]{2,1,0:T(8,128)S(1)} collective-permute-done((f32[8,128,128]{2,1,0:T(8,128)S(1)}, f32[8,128,128]{2,1,0:T(8,128)S(1)}, u32[]{:S(2)}, u32[]{:S(2)}) %collective-permute-start) | collective-permute-done | bytes 524320 | tf_op jit(solution)/shard_map/while/body/eval_jaxpr/ppermute | solution.py:14
  328.0 10.7 %collective-permute-done = f32[8,128,128]{2,1,0:T(8,128)S(1)} collective-permute-done((f32[8,128,128]{2,1,0:T(8,128)S(1)}, f32[8,128,128]{2,1,0:T(8,128)S(1)}, u32[]{:S(2)}, u32[]{:S(2)}) %collective-permute-start) | collective-permute-done | bytes 524320 | tf_op jit(solution)/shard_map/while/body/eval_jaxpr/ppermute | solution.py:14
  340.7 10.7 %collective-permute-done = f32[8,128,128]{2,1,0:T(8,128)S(1)} collective-permute-done((f32[8,128,128]{2,1,0:T(8,128)S(1)}, f32[8,128,128]{2,1,0:T(8,128)S(1)}, u32[]{:S(2)}, u32[]{:S(2)}) %collective-permute-start) | collective-permute-done | bytes 524320 | tf_op jit(solution)/shard_map/while/body/eval_jaxpr/ppermute | solution.py:14
  353.3 10.7 %collective-permute-done = f32[8,128,128]{2,1,0:T(8,128)S(1)} collective-permute-done((f32[8,128,128]{2,1,0:T(8,128)S(1)}, f32[8,128,128]{2,1,0:T(8,128)S(1)}, u32[]{:S(2)}, u32[]{:S(2)}) %collective-permute-start) | collective-permute-done | bytes 524320 | tf_op jit(solution)/shard_map/while/body/eval_jaxpr/ppermute | solution.py:14
  366.0 10.7 %collective-permute-done = f32[8,128,128]{2,1,0:T(8,128)S(1)} collective-permute-done((f32[8,128,128]{2,1,0:T(8,128)S(1)}, f32[8,128,128]{2,1,0:T(8,128)S(1)}, u32[]{:S(2)}, u32[]{:S(2)}) %collective-permute-start) | collective-permute-done | bytes 524320 | tf_op jit(solution)/shard_map/while/body/eval_jaxpr/ppermute | solution.py:14
  378.7 10.7 %collective-permute-done = f32[8,128,128]{2,1,0:T(8,128)S(1)} collective-permute-done((f32[8,128,128]{2,1,0:T(8,128)S(1)}, f32[8,128,128]{2,1,0:T(8,128)S(1)}, u32[]{:S(2)}, u32[]{:S(2)}) %collective-permute-start) | collective-permute-done | bytes 524320 | tf_op jit(solution)/shard_map/while/body/eval_jaxpr/ppermute | solution.py:14
  553.9 49.4 %all_to_all.50 = bf16[1024,8,128]{2,1,0:T(8,128)(2,1)} all-to-all(bf16[1024,8,128]{2,1,0:T(8,128)(2,1)S(1)} %bitcast.74), channel_id=1, replica_groups=mesh['seq'=32,'head'=8] {'head'}, dimensions={0} | all-to-all | bytes 4194304 | tf_op jit(solution)/shard_map/all_to_all | solution.py:75
  (118 shorter events, 259.4 us)
Async XLA Ops:
  8.4 59.7 %all-to-all-start = ((bf16[8,128,8,128]{3,2,1,0:T(8,128)(2,1)}), bf16[8,128,8,128]{3,2,1,0:T(8,128)(2,1)S(1)}, u32[]{:S(2)}, u32[]{:S(2)}) async-start(bf16[8,128,8,128]{3,2,1,0:T(8,128)(2,1)} %fusion.20), calls=%async_computation | async-start | bytes 4194304 | tf_op jit(solution)/shard_map/all_to_all | solution.py:51
  68.0 56.0 %all-to-all-start.1 = ((bf16[128,64,128]{2,0,1:T(8,128)(2,1)}), bf16[128,64,128]{2,0,1:T(8,128)(2,1)}, u32[]{:S(2)}, u32[]{:S(2)}) async-start(bf16[128,64,128]{2,0,1:T(8,128)(2,1)} %copy.40), calls=%async_computation.1 | async-start | bytes 4194304 | tf_op jit(solution)/shard_map/all_to_all | solution.py:49
  124.0 405.7 %all-to-all-start.2 = ((bf16[128,64,128]{2,0,1:T(8,128)(2,1)}), bf16[128,64,128]{2,0,1:T(8,128)(2,1)}, u32[]{:S(2)}, u32[]{:S(2)}) async-start(bf16[128,64,128]{2,0,1:T(8,128)(2,1)} %copy.48), calls=%async_computation.2 | async-start | bytes 4194304 | tf_op jit(solution)/shard_map/all_to_all | solution.py:48
  136.0 12.6 %collective-permute-start = (f32[8,128,128]{2,1,0:T(8,128)S(1)}, f32[8,128,128]{2,1,0:T(8,128)S(1)}, u32[]{:S(2)}, u32[]{:S(2)}) collective-permute-start(f32[8,128,128]{2,1,0:T(8,128)S(1)} %add.47), channel_id=1, source_target_pairs={{0,8},{8,16},{16,24},{24,32},{32,40},{40,48},{48,56},{56,64},{64,7... | collective-permute-start | bytes 1572872 | tf_op jit(solution)/shard_map/while/body/eval_jaxpr/ppermute | solution.py:14
  148.7 12.6 %collective-permute-start = (f32[8,128,128]{2,1,0:T(8,128)S(1)}, f32[8,128,128]{2,1,0:T(8,128)S(1)}, u32[]{:S(2)}, u32[]{:S(2)}) collective-permute-start(f32[8,128,128]{2,1,0:T(8,128)S(1)} %add.47), channel_id=1, source_target_pairs={{0,8},{8,16},{16,24},{24,32},{32,40},{40,48},{48,56},{56,64},{64,7... | collective-permute-start | bytes 1572872 | tf_op jit(solution)/shard_map/while/body/eval_jaxpr/ppermute | solution.py:14
  161.3 12.6 %collective-permute-start = (f32[8,128,128]{2,1,0:T(8,128)S(1)}, f32[8,128,128]{2,1,0:T(8,128)S(1)}, u32[]{:S(2)}, u32[]{:S(2)}) collective-permute-start(f32[8,128,128]{2,1,0:T(8,128)S(1)} %add.47), channel_id=1, source_target_pairs={{0,8},{8,16},{16,24},{24,32},{32,40},{40,48},{48,56},{56,64},{64,7... | collective-permute-start | bytes 1572872 | tf_op jit(solution)/shard_map/while/body/eval_jaxpr/ppermute | solution.py:14
  174.0 12.6 %collective-permute-start = (f32[8,128,128]{2,1,0:T(8,128)S(1)}, f32[8,128,128]{2,1,0:T(8,128)S(1)}, u32[]{:S(2)}, u32[]{:S(2)}) collective-permute-start(f32[8,128,128]{2,1,0:T(8,128)S(1)} %add.47), channel_id=1, source_target_pairs={{0,8},{8,16},{16,24},{24,32},{32,40},{40,48},{48,56},{56,64},{64,7... | collective-permute-start | bytes 1572872 | tf_op jit(solution)/shard_map/while/body/eval_jaxpr/ppermute | solution.py:14
  186.7 12.6 %collective-permute-start = (f32[8,128,128]{2,1,0:T(8,128)S(1)}, f32[8,128,128]{2,1,0:T(8,128)S(1)}, u32[]{:S(2)}, u32[]{:S(2)}) collective-permute-start(f32[8,128,128]{2,1,0:T(8,128)S(1)} %add.47), channel_id=1, source_target_pairs={{0,8},{8,16},{16,24},{24,32},{32,40},{40,48},{48,56},{56,64},{64,7... | collective-permute-start | bytes 1572872 | tf_op jit(solution)/shard_map/while/body/eval_jaxpr/ppermute | solution.py:14
  199.4 12.6 %collective-permute-start = (f32[8,128,128]{2,1,0:T(8,128)S(1)}, f32[8,128,128]{2,1,0:T(8,128)S(1)}, u32[]{:S(2)}, u32[]{:S(2)}) collective-permute-start(f32[8,128,128]{2,1,0:T(8,128)S(1)} %add.47), channel_id=1, source_target_pairs={{0,8},{8,16},{16,24},{24,32},{32,40},{40,48},{48,56},{56,64},{64,7... | collective-permute-start | bytes 1572872 | tf_op jit(solution)/shard_map/while/body/eval_jaxpr/ppermute | solution.py:14
  212.0 12.6 %collective-permute-start = (f32[8,128,128]{2,1,0:T(8,128)S(1)}, f32[8,128,128]{2,1,0:T(8,128)S(1)}, u32[]{:S(2)}, u32[]{:S(2)}) collective-permute-start(f32[8,128,128]{2,1,0:T(8,128)S(1)} %add.47), channel_id=1, source_target_pairs={{0,8},{8,16},{16,24},{24,32},{32,40},{40,48},{48,56},{56,64},{64,7... | collective-permute-start | bytes 1572872 | tf_op jit(solution)/shard_map/while/body/eval_jaxpr/ppermute | solution.py:14
  224.7 12.6 %collective-permute-start = (f32[8,128,128]{2,1,0:T(8,128)S(1)}, f32[8,128,128]{2,1,0:T(8,128)S(1)}, u32[]{:S(2)}, u32[]{:S(2)}) collective-permute-start(f32[8,128,128]{2,1,0:T(8,128)S(1)} %add.47), channel_id=1, source_target_pairs={{0,8},{8,16},{16,24},{24,32},{32,40},{40,48},{48,56},{56,64},{64,7... | collective-permute-start | bytes 1572872 | tf_op jit(solution)/shard_map/while/body/eval_jaxpr/ppermute | solution.py:14
  237.4 12.6 %collective-permute-start = (f32[8,128,128]{2,1,0:T(8,128)S(1)}, f32[8,128,128]{2,1,0:T(8,128)S(1)}, u32[]{:S(2)}, u32[]{:S(2)}) collective-permute-start(f32[8,128,128]{2,1,0:T(8,128)S(1)} %add.47), channel_id=1, source_target_pairs={{0,8},{8,16},{16,24},{24,32},{32,40},{40,48},{48,56},{56,64},{64,7... | collective-permute-start | bytes 1572872 | tf_op jit(solution)/shard_map/while/body/eval_jaxpr/ppermute | solution.py:14
  250.0 12.6 %collective-permute-start = (f32[8,128,128]{2,1,0:T(8,128)S(1)}, f32[8,128,128]{2,1,0:T(8,128)S(1)}, u32[]{:S(2)}, u32[]{:S(2)}) collective-permute-start(f32[8,128,128]{2,1,0:T(8,128)S(1)} %add.47), channel_id=1, source_target_pairs={{0,8},{8,16},{16,24},{24,32},{32,40},{40,48},{48,56},{56,64},{64,7... | collective-permute-start | bytes 1572872 | tf_op jit(solution)/shard_map/while/body/eval_jaxpr/ppermute | solution.py:14
  262.7 12.6 %collective-permute-start = (f32[8,128,128]{2,1,0:T(8,128)S(1)}, f32[8,128,128]{2,1,0:T(8,128)S(1)}, u32[]{:S(2)}, u32[]{:S(2)}) collective-permute-start(f32[8,128,128]{2,1,0:T(8,128)S(1)} %add.47), channel_id=1, source_target_pairs={{0,8},{8,16},{16,24},{24,32},{32,40},{40,48},{48,56},{56,64},{64,7... | collective-permute-start | bytes 1572872 | tf_op jit(solution)/shard_map/while/body/eval_jaxpr/ppermute | solution.py:14
  275.4 12.6 %collective-permute-start = (f32[8,128,128]{2,1,0:T(8,128)S(1)}, f32[8,128,128]{2,1,0:T(8,128)S(1)}, u32[]{:S(2)}, u32[]{:S(2)}) collective-permute-start(f32[8,128,128]{2,1,0:T(8,128)S(1)} %add.47), channel_id=1, source_target_pairs={{0,8},{8,16},{16,24},{24,32},{32,40},{40,48},{48,56},{56,64},{64,7... | collective-permute-start | bytes 1572872 | tf_op jit(solution)/shard_map/while/body/eval_jaxpr/ppermute | solution.py:14
  288.0 12.6 %collective-permute-start = (f32[8,128,128]{2,1,0:T(8,128)S(1)}, f32[8,128,128]{2,1,0:T(8,128)S(1)}, u32[]{:S(2)}, u32[]{:S(2)}) collective-permute-start(f32[8,128,128]{2,1,0:T(8,128)S(1)} %add.47), channel_id=1, source_target_pairs={{0,8},{8,16},{16,24},{24,32},{32,40},{40,48},{48,56},{56,64},{64,7... | collective-permute-start | bytes 1572872 | tf_op jit(solution)/shard_map/while/body/eval_jaxpr/ppermute | solution.py:14
  300.7 12.6 %collective-permute-start = (f32[8,128,128]{2,1,0:T(8,128)S(1)}, f32[8,128,128]{2,1,0:T(8,128)S(1)}, u32[]{:S(2)}, u32[]{:S(2)}) collective-permute-start(f32[8,128,128]{2,1,0:T(8,128)S(1)} %add.47), channel_id=1, source_target_pairs={{0,8},{8,16},{16,24},{24,32},{32,40},{40,48},{48,56},{56,64},{64,7... | collective-permute-start | bytes 1572872 | tf_op jit(solution)/shard_map/while/body/eval_jaxpr/ppermute | solution.py:14
  313.4 12.6 %collective-permute-start = (f32[8,128,128]{2,1,0:T(8,128)S(1)}, f32[8,128,128]{2,1,0:T(8,128)S(1)}, u32[]{:S(2)}, u32[]{:S(2)}) collective-permute-start(f32[8,128,128]{2,1,0:T(8,128)S(1)} %add.47), channel_id=1, source_target_pairs={{0,8},{8,16},{16,24},{24,32},{32,40},{40,48},{48,56},{56,64},{64,7... | collective-permute-start | bytes 1572872 | tf_op jit(solution)/shard_map/while/body/eval_jaxpr/ppermute | solution.py:14
  326.1 12.6 %collective-permute-start = (f32[8,128,128]{2,1,0:T(8,128)S(1)}, f32[8,128,128]{2,1,0:T(8,128)S(1)}, u32[]{:S(2)}, u32[]{:S(2)}) collective-permute-start(f32[8,128,128]{2,1,0:T(8,128)S(1)} %add.47), channel_id=1, source_target_pairs={{0,8},{8,16},{16,24},{24,32},{32,40},{40,48},{48,56},{56,64},{64,7... | collective-permute-start | bytes 1572872 | tf_op jit(solution)/shard_map/while/body/eval_jaxpr/ppermute | solution.py:14
  338.7 12.6 %collective-permute-start = (f32[8,128,128]{2,1,0:T(8,128)S(1)}, f32[8,128,128]{2,1,0:T(8,128)S(1)}, u32[]{:S(2)}, u32[]{:S(2)}) collective-permute-start(f32[8,128,128]{2,1,0:T(8,128)S(1)} %add.47), channel_id=1, source_target_pairs={{0,8},{8,16},{16,24},{24,32},{32,40},{40,48},{48,56},{56,64},{64,7... | collective-permute-start | bytes 1572872 | tf_op jit(solution)/shard_map/while/body/eval_jaxpr/ppermute | solution.py:14
  351.4 12.6 %collective-permute-start = (f32[8,128,128]{2,1,0:T(8,128)S(1)}, f32[8,128,128]{2,1,0:T(8,128)S(1)}, u32[]{:S(2)}, u32[]{:S(2)}) collective-permute-start(f32[8,128,128]{2,1,0:T(8,128)S(1)} %add.47), channel_id=1, source_target_pairs={{0,8},{8,16},{16,24},{24,32},{32,40},{40,48},{48,56},{56,64},{64,7... | collective-permute-start | bytes 1572872 | tf_op jit(solution)/shard_map/while/body/eval_jaxpr/ppermute | solution.py:14
  364.1 12.6 %collective-permute-start = (f32[8,128,128]{2,1,0:T(8,128)S(1)}, f32[8,128,128]{2,1,0:T(8,128)S(1)}, u32[]{:S(2)}, u32[]{:S(2)}) collective-permute-start(f32[8,128,128]{2,1,0:T(8,128)S(1)} %add.47), channel_id=1, source_target_pairs={{0,8},{8,16},{16,24},{24,32},{32,40},{40,48},{48,56},{56,64},{64,7... | collective-permute-start | bytes 1572872 | tf_op jit(solution)/shard_map/while/body/eval_jaxpr/ppermute | solution.py:14
  376.7 12.6 %collective-permute-start = (f32[8,128,128]{2,1,0:T(8,128)S(1)}, f32[8,128,128]{2,1,0:T(8,128)S(1)}, u32[]{:S(2)}, u32[]{:S(2)}) collective-permute-start(f32[8,128,128]{2,1,0:T(8,128)S(1)} %add.47), channel_id=1, source_target_pairs={{0,8},{8,16},{16,24},{24,32},{32,40},{40,48},{48,56},{56,64},{64,7... | collective-permute-start | bytes 1572872 | tf_op jit(solution)/shard_map/while/body/eval_jaxpr/ppermute | solution.py:14
  389.4 12.6 %collective-permute-start = (f32[8,128,128]{2,1,0:T(8,128)S(1)}, f32[8,128,128]{2,1,0:T(8,128)S(1)}, u32[]{:S(2)}, u32[]{:S(2)}) collective-permute-start(f32[8,128,128]{2,1,0:T(8,128)S(1)} %add.47), channel_id=1, source_target_pairs={{0,8},{8,16},{16,24},{24,32},{32,40},{40,48},{48,56},{56,64},{64,7... | collective-permute-start | bytes 1572872 | tf_op jit(solution)/shard_map/while/body/eval_jaxpr/ppermute | solution.py:14
  (16 other events, 149.8 us)
